TPU v7x, 256 devices: a whole 4x4x8 slice. The times are simulated.
256 devices in a mesh: doc: 64 (over x, z, core), feat: 4 (over y).
Axes of the slice: x: 4, y: 4, z: 8, core: 2. Of those that a mesh axis runs over, the one named last changes fastest.
Arguments:
- b_tiles: bfloat16 [12288, 512, 128], P('doc', 'feat'), may hold values from -0.0625 to 0.0625
- b_rows: int32 [12288, 4], P('doc', 'feat'), may hold values from 0 to 11, as said below
- b_cols: int32 [12288, 4], P('doc', 'feat'), may hold values from 0 to 4095
- b_count: int32 [64, 4], P('doc', 'feat'), may hold values from 144 to 192
- b_offsets: int32 [65], replicated, may hold values from 0 to 480, as said below
- a_tiles: bfloat16 [4096, 512, 128], P('doc', 'feat'), may hold values from -0.375 to 0.375
- a_rows: int32 [4096, 4], P('doc', 'feat'), may hold values from 0 to 12, as said below
- a_tags: int32 [4096, 4], P('doc', 'feat'), may hold values from 0 to 8191, as said below
- a_count: int32 [64, 4], P('doc', 'feat'), may hold values from 48 to 64
- a_offsets: int32 [65], replicated, may hold values from 0 to 480, as said below
- omega_seed: int32 [1], replicated, may hold values from 0 to 1073741823
Outputs:
- tag_sketch: float32 [1048576, 256], P(('doc', 'feat'))
Inputs may be any that keep to these rules, and one draw needn't show every extreme that they name: b_offsets[0] is 0 and each device's range of the text view holds 3 to 12 row blocks. a_offsets[0] is 0 and a_offsets[64] equals b_offsets[64]; every other entry lies 1 to 2 row blocks below the same entry of b_offsets; each device's range of the tag view holds at most 13 row blocks. `b_rows`: below the number of row blocks of the device's range of the text view. `a_rows`: below the number of row blocks of the device's range of the tag view. `a_tags`: the rows of a tile's tag block lie, under the output's placement, on a device with the same feat index as the tile; on one device at most 2 tiles in use have tag blocks on devices of one doc index, and in every draw some doc index gets exactly 2 tiles in use from every device.
All inputs are finite; a program needn't handle non-finite values.
Results may differ from a plain program's by a relative error of at most 0.004.
Values may be sent and summed in bfloat16 or wider, within the bound.
A program may use at most 128 MiB of HBM per device.

v0:
```python
import jax
import jax.numpy as jnp
from jax import lax
from jax.sharding import PartitionSpec as P

TILE = 128
SKETCH = 256
TERMS = 2097152
TAG_DEV = 4096
ROWB_MAX = 12
MARGIN = 2
ROWA_MAX = 13


def passed_along(block, axis, distance):
    devices = range(lax.axis_size(axis))
    route = [(i - distance, i) for i in devices if i - distance in devices]
    return lax.ppermute(block, axis, route)


def unsigned_shift(value, count):
    return lax.shift_right_logical(value, jnp.full(value.shape, count, jnp.int32))


def omega_panel(term_blocks, seed_value):
    row_iota = lax.broadcasted_iota(jnp.int32, (1, TILE, SKETCH), 1)
    col_iota = lax.broadcasted_iota(jnp.int32, (1, TILE, SKETCH), 2)
    mixing = (term_blocks[:, None, None] * TILE + row_iota) * SKETCH + col_iota
    mixing = mixing ^ seed_value * 747796405
    mixing = mixing ^ unsigned_shift(mixing, 16)
    mixing = mixing * 2146121005
    mixing = mixing ^ unsigned_shift(mixing, 15)
    mixing = mixing * -2073254261
    mixing = mixing ^ unsigned_shift(mixing, 16)
    levels = (unsigned_shift(mixing, 8) & 65535).astype(jnp.float32)
    return ((levels - 32767.5) * (3.4641016 / 65536.0)).astype(jnp.bfloat16)


def local(
    b_tiles,
    b_rows,
    b_cols,
    b_count,
    b_offsets,
    a_tiles,
    a_rows,
    a_tags,
    a_count,
    a_offsets,
    omega_seed,
):
    doc_count = lax.axis_size("doc")
    feat_count = lax.axis_size("feat")
    doc_here = lax.axis_index("doc")
    feat_here = lax.axis_index("feat")
    tiles_b = b_tiles.shape[0]
    tiles_a = a_tiles.shape[0]
    highest = lax.Precision.HIGHEST
    slab_blocks = TERMS // (TILE * feat_count)
    panels = omega_panel(b_cols[:, 0] + feat_here * slab_blocks, omega_seed[0])
    tile_terms = jnp.einsum("tij,tjk->tik", b_tiles, panels, preferred_element_type=jnp.float32)
    live_b = jnp.arange(tiles_b, dtype=jnp.int32) < b_count[0, 0]
    chosen = (b_rows[:, 0][None, :] == jnp.arange(ROWB_MAX, dtype=jnp.int32)[:, None]) & live_b[
        None, :
    ]
    partial_value = jnp.einsum(
        "rt,tik->rik", chosen.astype(jnp.float32), tile_terms, precision=highest
    )
    b_start = b_offsets[doc_here]
    b_length = b_offsets[doc_here + 1] - b_start
    shift_rows = a_offsets[doc_here] - b_start + MARGIN
    own_rows = lax.psum(partial_value, "feat").astype(jnp.bfloat16)
    last_rows = lax.dynamic_slice_in_dim(own_rows, b_length - MARGIN, MARGIN, 0)
    arrived = passed_along(last_rows, "doc", 1)
    source = jnp.concatenate([arrived, own_rows], axis=0)
    row_picks = jnp.clip(
        jnp.arange(ROWA_MAX, dtype=jnp.int32) + shift_rows, 0, MARGIN + ROWB_MAX - 1
    )
    z_rows = jnp.take(source, row_picks, axis=0)
    live_a = jnp.arange(tiles_a, dtype=jnp.int32) < a_count[0, 0]
    tile_rows = jnp.take(z_rows, a_rows[:, 0], axis=0)
    tag_blocks = a_tags[:, 0]
    owned_blocks = TAG_DEV // TILE
    capacity = max(2, (tiles_a + doc_count - 1) // doc_count)
    owner_doc = tag_blocks // owned_blocks // feat_count
    owner_hits = (
        (owner_doc[:, None] == jnp.arange(doc_count, dtype=jnp.int32)[None, :]) & live_a[:, None]
    ).astype(jnp.int32)
    earlier = jnp.cumsum(owner_hits, axis=0) - owner_hits
    ranking = jnp.sum(earlier * owner_hits, axis=1)
    slot_index = jnp.where(live_a, owner_doc * capacity + ranking, doc_count * capacity)
    sent_ids = (
        jnp.full((doc_count * capacity,), -1, jnp.int32)
        .at[slot_index]
        .set(tag_blocks, mode="drop")
        .reshape(doc_count, capacity)
    )
    products = jnp.einsum("tij,tik->tjk", a_tiles, tile_rows, preferred_element_type=jnp.float32)
    outbox = (
        jnp.zeros((doc_count * capacity, TILE, SKETCH), jnp.float32)
        .at[slot_index]
        .set(products, mode="drop")
    )
    arrived_sums, arrived_ids = (
        lax.all_to_all(
            outbox.reshape(doc_count, capacity, TILE, SKETCH),
            "doc",
            split_axis=0,
            concat_axis=0,
            tiled=True,
        ),
        lax.all_to_all(sent_ids, "doc", split_axis=0, concat_axis=0, tiled=True),
    )
    flat_here = doc_here * feat_count + feat_here
    local_blocks = arrived_ids.reshape(-1) - flat_here * owned_blocks
    block_pick = (
        jnp.arange(owned_blocks, dtype=jnp.int32)[:, None] == local_blocks[None, :]
    ).astype(jnp.float32)
    sketch = jnp.einsum(
        "bs,sjk->bjk", block_pick, arrived_sums.reshape(-1, TILE, SKETCH), precision=highest
    )
    return sketch.reshape(TAG_DEV, SKETCH)


def solution(mesh):
    return jax.shard_map(
        local,
        mesh=mesh,
        in_specs=(
            P("doc", "feat", None),
            P("doc", "feat"),
            P("doc", "feat"),
            P("doc", "feat"),
            P(),
            P("doc", "feat", None),
            P("doc", "feat"),
            P("doc", "feat"),
            P("doc", "feat"),
            P(),
            P(),
        ),
        out_specs=P(("doc", "feat"), None),
        check_vma=False,
    )
```

profile of v0, /device:TPU:1, one launch (start us, length us, event | category | flops | bytes accessed | tf_op | source)
XLA Modules:
  0.0 622.7 jit_solution(13340459511408527445)
XLA Ops:
  0.0 0.0 copy-start
  0.0 1.4 fusion.58
  3.3 0.7 add_multiply_fusion
  4.0 18.3 %fusion.21 = f32[192,128,256]{1,2,0:T(8,128)} fusion(bf16[192,128,128]{2,1,0:T(8,128)(2,1)} %param.11, s32[]{:T(128)} %bitcast.13, s32[192]{0:T(256)S(1)} %bitcast.49), kind=kOutput, calls=%fused_computation.27 | convolution fusion | flops 1723858944 | bytes 31458052 | tf_op jit(solution)/shard_map/tij,tjk->tik/dot_general | solution.py:61
  22.3 0.0 copy-start.2
  22.3 24.8 %copy.21 = f32[192,128,256]{2,0,1:T(8,128)} copy(f32[192,128,256]{1,2,0:T(8,128)} %fusion.21) | data formatting | bytes 50331648 | tf_op jit(solution)/shard_map/tij,tjk->tik/dot_general | solution.py:61
  47.2 0.0 copy-start.3
  47.2 0.0 copy-start.4
  47.2 0.0 copy-start.5
  47.9 0.0 copy-done.2
  47.9 13.5 %fusion.38 = f32[12,128,256]{2,0,1:T(8,128)} fusion(f32[192,128,256]{2,0,1:T(8,128)} %copy.21, s32[192]{0:T(256)S(1)} %bitcast.48, pred[192]{0:T(512)(128)(4,1)S(1)} %iota_compare_fusion.3), kind=kOutput, calls=%fused_computation.46 | convolution fusion | flops 905974272 | bytes 26739648 | tf_op jit(solution)/shard_map/rt,tik->rik/dot_general | solution.py:66
  61.4 43.2 %all-reduce.1 = bf16[12,128,256]{2,0,1:T(8,128)(2,1)S(1)} all-reduce(f32[12,128,256]{2,0,1:T(8,128)} %fusion.38), channel_id=1, replica_groups=mesh['doc'=64,'feat'=4] {'feat'}, use_global_device_ids=true, to_apply=%region_3.4 | all-reduce | flops 393216 | bytes 2359296 | tf_op jit(solution)/shard_map/psum | solution.py:72
  104.7 0.2 constant_dynamic-slice_fusion
  104.9 5.5 collective-permute-start
  111.1 0.0 copy-done.3
  111.1 0.1 fusion.32
  111.2 0.1 reduce_window_sum.11
  111.3 0.2 select_reduce_fusion
  111.5 0.8 scatter_custom_fusion
  112.3 0.7 all_to_all.9
  113.0 10.7 %all-to-all-start = ((s32[64,1,2]{2,1,0:T(1,128)}), s32[64,1,2]{2,1,0:T(1,128)S(1)}, u32[]{:S(2)}, u32[]{:S(2)}) async-start(s32[64,1,2]{2,1,0:T(1,128)} %bitcast.5), calls=%async_computation | async-start | bytes 65536 | tf_op jit(solution)/shard_map/all_to_all | solution.py:112
  123.7 0.0 copy-done.4
  123.8 0.0 copy-done.5
  123.8 0.6 dynamic_slice.12
  125.7 0.0 collective-permute-done
  125.7 0.5 pad_maximum_fusion
  126.2 0.3 copy.22
  126.5 1.5 gather_fusion
  128.0 1.3 broadcast_select_fusion
  129.3 2.8 gather_fusion.1
  132.2 0.0 copy-done
  132.2 6.8 %fusion.27 = f32[64,128,256]{1,2,0:T(8,128)} fusion(bf16[64,128,128]{2,1,0:T(8,128)(2,1)S(1)} %copy-done, bf16[64,128,256]{2,1,0:T(8,128)(2,1)} %gather_fusion.1, pred[64]{0:T(512)(128)(4,1)S(1)} %and_bitcast_fusion), kind=kOutput, calls=%fused_computation.31 | convolution fusion | flops 538968064 | bytes 14680128 | tf_op jit(solution)/shard_map/tij,tik->tjk/dot_general | solution.py:98
  138.9 9.0 %copy.24 = f32[64,128,256]{2,1,0:T(8,128)} copy(f32[64,128,256]{1,2,0:T(8,128)} %fusion.27) | data formatting | bytes 16777216 | tf_op jit(solution)/shard_map/tij,tik->tjk/dot_general | solution.py:98
  147.9 7.8 %broadcast_in_dim.48 = f32[128,128,256]{2,1,0:T(8,128)} broadcast(f32[]{:T(128)} %constant.99.clone.1), dimensions={} | broadcast | bytes 16777220 | tf_op jit(solution)/shard_map/broadcast_in_dim | solution.py:100
  155.8 16.0 %scatter_fusion = f32[128,128,256]{2,1,0:T(8,128)} fusion(f32[128,128,256]{2,1,0:T(8,128)} %broadcast_in_dim.48, s32[64]{0:T(128)S(1)} %fusion.44, f32[64,128,256]{2,1,0:T(8,128)} %copy.24), kind=kCustom, calls=%fused_computation.3 | custom fusion | bytes 25166080 | tf_op jit(solution)/shard_map/scatter | solution.py:102
  171.8 28.5 %copy.25 = f32[64,2,128,256]{3,1,2,0:T(2,128)} copy(f32[64,2,128,256]{3,2,1,0:T(8,128)} %bitcast.47) | data formatting | bytes 33554432 | tf_op jit(solution)/shard_map/reshape | solution.py:106
  200.3 0.0 all-to-all-done
  200.3 10.3 %all-to-all-start.1 = ((f32[64,2,128,256]{3,1,2,0:T(2,128)}), f32[64,2,128,256]{3,1,2,0:T(2,128)}, u32[]{:S(2)}, u32[]{:S(2)}) async-start(f32[64,2,128,256]{3,1,2,0:T(2,128)} %copy.25), calls=%async_computation.1 | async-start | bytes 33554432 | tf_op jit(solution)/shard_map/all_to_all | solution.py:105
  210.6 0.1 subtract_reduce_fusion
  210.7 0.1 sub.48
  210.8 365.2 %all-to-all-done.1 = f32[64,2,128,256]{3,1,2,0:T(2,128)} async-done(((f32[64,2,128,256]{3,1,2,0:T(2,128)}), f32[64,2,128,256]{3,1,2,0:T(2,128)}, u32[]{:S(2)}, u32[]{:S(2)}) %all-to-all-start.1) | async-done | bytes 16777248 | tf_op jit(solution)/shard_map/all_to_all | solution.py:105
  576.1 12.1 %copy.26 = f32[64,2,128,256]{3,1,0,2:T(2,128)} copy(f32[64,2,128,256]{3,1,2,0:T(2,128)} %all-to-all-done.1) | data formatting | bytes 33554432 | tf_op jit(solution)/shard_map/all_to_all | solution.py:105
  588.2 0.0 copy-start.1
  588.2 20.7 %reshape.87 = f32[128,128,256]{2,0,1:T(8,128)} reshape(f32[64,2,128,256]{3,1,0,2:T(2,128)} %copy.26) | data formatting | bytes 33554432 | tf_op jit(solution)/shard_map/reshape | solution.py:120
  608.9 9.4 %fusion.34 = f32[32,128,256]{2,0,1:T(8,128)S(1)} fusion(f32[128,128,256]{2,0,1:T(8,128)} %reshape.87, s32[128]{0:T(128)S(1)} %sub.48), kind=kOutput, calls=%fused_computation.43 | convolution fusion | flops 1610616832 | bytes 20972032 | tf_op jit(solution)/shard_map/bs,sjk->bjk/dot_general | solution.py:119
  618.3 4.4 copy.27
  622.7 0.0 copy-done.1
  (10 shorter events, 0.1 us)
Async XLA Ops:
  0.0 132.2 %copy-start = (bf16[64,128,128]{2,1,0:T(8,128)(2,1)S(1)}, bf16[64,128,128]{2,1,0:T(8,128)(2,1)}, u32[]{:S(2)}) copy-start(bf16[64,128,128]{2,1,0:T(8,128)(2,1)} %param.16) | copy-start | bytes 6291460
  22.3 25.6 %copy-start.2 = (s32[192,1]{0,1:T(1,128)S(1)}, s32[192,1]{0,1:T(1,128)}, u32[]{:S(2)}) copy-start(s32[192,1]{0,1:T(1,128)} %param.12) | copy-start | bytes 2308
  47.2 63.9 %copy-start.3 = (s32[64,1]{0,1:T(1,128)S(1)}, s32[64,1]{0,1:T(1,128)}, u32[]{:S(2)}) copy-start(s32[64,1]{0,1:T(1,128)} %param.18) | copy-start | bytes 772
  47.2 76.5 %copy-start.4 = (s32[64,1]{0,1:T(1,128)S(1)}, s32[64,1]{0,1:T(1,128)}, u32[]{:S(2)}) copy-start(s32[64,1]{0,1:T(1,128)} %param.17) | copy-start | bytes 772
  47.2 76.6 %copy-start.5 = (s32[65]{0:T(128)S(1)}, s32[65]{0:T(128)}, u32[]{:S(2)}) copy-start(s32[65]{0:T(128)} %param.20) | copy-start | bytes 784
  104.9 20.8 %collective-permute-start = (bf16[2,128,256]{2,0,1:T(2,128)(2,1)S(1)}, bf16[2,128,256]{2,0,1:T(2,128)(2,1)S(1)}, u32[]{:S(2)}, u32[]{:S(2)}) collective-permute-start(bf16[2,128,256]{2,0,1:T(2,128)(2,1)S(1)} %constant_dynamic-slice_fusion), channel_id=1, source_target_pairs={{0,4},{4,8},{8,12},{12,16},{16,20},{20,24},{24,28},{28,32},{32,36}... | collective-permute-start | bytes 393224 | tf_op jit(solution)/shard_map/ppermute | solution.py:18
  113.0 87.3 %all-to-all-start = ((s32[64,1,2]{2,1,0:T(1,128)}), s32[64,1,2]{2,1,0:T(1,128)S(1)}, u32[]{:S(2)}, u32[]{:S(2)}) async-start(s32[64,1,2]{2,1,0:T(1,128)} %bitcast.5), calls=%async_computation | async-start | bytes 65536 | tf_op jit(solution)/shard_map/all_to_all | solution.py:112
  200.3 375.8 %all-to-all-start.1 = ((f32[64,2,128,256]{3,1,2,0:T(2,128)}), f32[64,2,128,256]{3,1,2,0:T(2,128)}, u32[]{:S(2)}, u32[]{:S(2)}) async-start(f32[64,2,128,256]{3,1,2,0:T(2,128)} %copy.25), calls=%async_computation.1 | async-start | bytes 33554432 | tf_op jit(solution)/shard_map/all_to_all | solution.py:105
  588.2 34.5 %copy-start.1 = (bf16[64,128,128]{2,1,0:T(8,128)(2,1)S(1)}, bf16[64,128,128]{2,1,0:T(8,128)(2,1)}, u32[]{:S(2)}) copy-start(bf16[64,128,128]{2,1,0:T(8,128)(2,1)} %param.16) | copy-start | bytes 6291460
where the time goes:
time: 624 us; the launch traced here: 623 us
  waiting for transfers between devices  365 us (58%)
  local copies, waits for them, and re-layouts  132 us (21%)
  matrix products  48 us (8%)
  blocking collectives  43.2 us (7%)
  starting transfers between devices  26.6 us (4%)
    all_to_all x1, waiting for transfers between devices, local(): lax.all_to_all(outbox.reshape(doc_count, capacity, TILE, SKETCH), 'doc',...  365 us
    psum x1, blocking collectives, local(): own_rows = lax.psum(partial_value, 'feat').astype(jnp.bfloat16)  43.2 us
    reshape x1, local copies, waits for them, and re-layouts, local(): outbox.reshape(doc_count, capacity, TILE, SKETCH)  28.5 us
    dot_general x1, local copies, waits for them, and re-layouts, local(): jnp.einsum('tij,tjk->tik', b_tiles, panels, preferred_element_type=jnp.fl...  24.8 us
    reshape x1, local copies, waits for them, and re-layouts, local(): arrived_sums.reshape(-1, TILE, SKETCH)  20.7 us
    dot_general x1, matrix products, local(): jnp.einsum('tij,tjk->tik', b_tiles, panels, preferred_element_type=jnp.fl...  18.3 us
    scatter x1, local copies, waits for them, and re-layouts, local(): outbox = jnp.zeros((doc_count * capacity, TILE, SKETCH), jnp.float32).at[...  16 us
    dot_general x1, matrix products, local(): jnp.einsum('rt,tik->rik', chosen.astype(jnp.float32), tile_terms, precisi...  13.5 us
  transfers between devices with their start and end apart: 3, of which 1 were waited for; matrix products, arithmetic and copies ran while one was open for 12% of the time, Pallas kernels for 0%

commit v1 on v0

--- a/solution.py
+++ b/solution.py
@@ -10,6 +10,10 @@
 ROWB_MAX = 12
 MARGIN = 2
 ROWA_MAX = 13
+
+
+def begin_the_body(inner_x):
+    return jnp.sum(lax.all_gather(inner_x, "feat"), 0)
 
 
 def passed_along(block, axis, distance):
@@ -69,7 +73,7 @@
     b_start = b_offsets[doc_here]
     b_length = b_offsets[doc_here + 1] - b_start
     shift_rows = a_offsets[doc_here] - b_start + MARGIN
-    own_rows = lax.psum(partial_value, "feat").astype(jnp.bfloat16)
+    own_rows = begin_the_body(partial_value).astype(jnp.bfloat16)
     last_rows = lax.dynamic_slice_in_dim(own_rows, b_length - MARGIN, MARGIN, 0)
     arrived = passed_along(last_rows, "doc", 1)
     source = jnp.concatenate([arrived, own_rows], axis=0)

time: 624 us -> 657 us (1.053)
  waiting for transfers between devices: 365 us -> 420 us
  blocking collectives: 43.2 us -> 0 us
  between operations: 4.73 us -> 18.3 us
    all_gather x0 -> x1, waiting for transfers between devices: none -> 52.6 us  [begin_the_body(): return jnp.sum(lax.all_gather(inner_x, 'feat'), 0)]
    psum x1 -> x0, blocking collectives: 43.2 us -> none  [local(): own_rows = lax.psum(partial_value, 'feat').astype(jnp.bfloat16)]
  transfers between devices with their start and end apart: 3 -> 4, of which waited for: 1 -> 3; matrix products, arithmetic and copies ran while one was open for 12% -> 13% of each run, Pallas kernels for 0% -> 0%
where the time goes in v1:
time: 657 us; the launch traced here: 656 us
  waiting for transfers between devices  420 us (64%)
  local copies, waits for them, and re-layouts  134 us (20%)
  matrix products  47.3 us (7%)
  starting transfers between devices  29.5 us (4%)
  between operations  18.3 us (3%)
  other arithmetic  6.88 us (1%)
    all_to_all x1, waiting for transfers between devices, local(): lax.all_to_all(outbox.reshape(doc_count, capacity, TILE, SKETCH), 'doc',...  365 us
    all_gather x1, waiting for transfers between devices, begin_the_body(): return jnp.sum(lax.all_gather(inner_x, 'feat'), 0)  52.6 us
    reshape x1, local copies, waits for them, and re-layouts, local(): outbox.reshape(doc_count, capacity, TILE, SKETCH)  28.5 us
    dot_general x1, local copies, waits for them, and re-layouts, local(): jnp.einsum('tij,tjk->tik', b_tiles, panels, preferred_element_type=jnp.fl...  24.9 us
    reshape x1, local copies, waits for them, and re-layouts, local(): arrived_sums.reshape(-1, TILE, SKETCH)  20.7 us
    dot_general x1, matrix products, local(): jnp.einsum('tij,tjk->tik', b_tiles, panels, preferred_element_type=jnp.fl...  18.3 us
    scatter x1, local copies, waits for them, and re-layouts, local(): outbox = jnp.zeros((doc_count * capacity, TILE, SKETCH), jnp.float32).at[...  16.1 us
  transfers between devices with their start and end apart: 4, of which 3 were waited for; matrix products, arithmetic and copies ran while one was open for 13% of the time, Pallas kernels for 0%

profile of v1, /device:TPU:1, one launch (start us, length us, event | category | flops | bytes accessed | tf_op | source)
XLA Modules:
  0.0 655.7 jit_solution(7076331839579209409)
XLA Ops:
  6.5 0.0 copy-start
  6.5 0.0 all-gather.3.cloned.1.call-start
  7.3 0.7 add_multiply_fusion
  8.0 18.3 %fusion.21 = f32[192,128,256]{1,2,0:T(8,128)} fusion(bf16[192,128,128]{2,1,0:T(8,128)(2,1)} %param.11, s32[]{:T(128)} %bitcast.13, s32[192]{0:T(256)S(1)} %bitcast.51), kind=kOutput, calls=%fused_computation.27 | convolution fusion | flops 1723858944 | bytes 31458052 | tf_op jit(solution)/shard_map/tij,tjk->tik/dot_general | solution.py:65
  26.3 0.0 copy-start.3
  26.3 24.9 %copy.20 = f32[192,128,256]{2,0,1:T(8,128)} copy(f32[192,128,256]{1,2,0:T(8,128)} %fusion.21) | data formatting | bytes 50331648 | tf_op jit(solution)/shard_map/tij,tjk->tik/dot_general | solution.py:65
  51.2 0.0 copy-start.4
  51.2 0.0 copy-start.2
  51.2 0.0 copy-start.5
  51.2 0.0 copy-start.6
  51.9 0.0 copy-done.3
  52.0 12.8 %fusion.38 = f32[12,128,256]{2,0,1:T(8,128)S(1)} fusion(f32[192,128,256]{2,0,1:T(8,128)} %copy.20, s32[192]{0:T(256)S(1)} %bitcast.50, pred[192]{0:T(512)(128)(4,1)S(1)} %iota_compare_fusion.3), kind=kOutput, calls=%fused_computation.46 | convolution fusion | flops 905974272 | bytes 26739648 | tf_op jit(solution)/shard_map/rt,tik->rik/dot_general | solution.py:70
  64.8 2.1 copy.21
  66.8 0.0 all-gather.3.cloned.1.call-update
  67.5 0.0 copy-done.4
  67.6 0.1 fusion.32
  67.7 0.1 reduce_window_sum.11
  67.7 0.2 select_reduce_fusion
  68.0 0.8 scatter_custom_fusion
  68.7 0.7 all_to_all.9
  69.5 13.0 %all-to-all-start = ((s32[64,1,2]{2,1,0:T(1,128)}), s32[64,1,2]{2,1,0:T(1,128)S(1)}, u32[]{:S(2)}, u32[]{:S(2)}) async-start(s32[64,1,2]{2,1,0:T(1,128)} %bitcast.5), calls=%async_computation | async-start | bytes 65536 | tf_op jit(solution)/shard_map/all_to_all | solution.py:116
  82.5 0.0 copy-done.2
  82.5 0.7 fusion.58
  84.4 0.0 copy-done.5
  84.4 0.6 dynamic_slice.12
  86.3 0.0 copy-done.6
  86.3 52.6 %all-gather.3.cloned.1.call-done = f32[48,128,256]{2,1,0:T(8,128)} async-done(((f32[12,128,256]{2,1,0:T(8,128)}), f32[48,128,256]{2,1,0:T(8,128)}) %all-gather.3.cloned.1.call-update) | async-done | bytes 6291472 | tf_op jit(solution)/shard_map/all_gather | solution.py:16
  138.9 3.4 reduce_sum.22
  142.3 3.9 collective-permute-start
  146.2 1.9 collective-permute-done
  148.1 1.0 pad_maximum_fusion
  149.1 2.7 gather_fusion
  151.8 1.3 broadcast_select_fusion
  153.1 2.8 gather_fusion.1
  155.9 0.0 copy-done
  155.9 6.8 %fusion.27 = f32[64,128,256]{1,2,0:T(8,128)} fusion(bf16[64,128,128]{2,1,0:T(8,128)(2,1)S(1)} %copy-done, bf16[64,128,256]{2,1,0:T(8,128)(2,1)} %gather_fusion.1, pred[64]{0:T(512)(128)(4,1)S(1)} %and_bitcast_fusion), kind=kOutput, calls=%fused_computation.31 | convolution fusion | flops 538968064 | bytes 14680128 | tf_op jit(solution)/shard_map/tij,tik->tjk/dot_general | solution.py:102
  162.7 9.0 %copy.23 = f32[64,128,256]{2,1,0:T(8,128)} copy(f32[64,128,256]{1,2,0:T(8,128)} %fusion.27) | data formatting | bytes 16777216 | tf_op jit(solution)/shard_map/tij,tik->tjk/dot_general | solution.py:102
  171.7 7.8 %broadcast_in_dim.48 = f32[128,128,256]{2,1,0:T(8,128)} broadcast(f32[]{:T(128)} %constant.100.clone.1), dimensions={} | broadcast | bytes 16777220 | tf_op jit(solution)/shard_map/broadcast_in_dim | solution.py:104
  179.5 16.1 %scatter_fusion = f32[128,128,256]{2,1,0:T(8,128)} fusion(f32[128,128,256]{2,1,0:T(8,128)} %broadcast_in_dim.48, s32[64]{0:T(128)S(1)} %fusion.44, f32[64,128,256]{2,1,0:T(8,128)} %copy.23), kind=kCustom, calls=%fused_computation.3 | custom fusion | bytes 25166080 | tf_op jit(solution)/shard_map/scatter | solution.py:106
  195.6 28.5 %copy.24 = f32[64,2,128,256]{3,1,2,0:T(2,128)} copy(f32[64,2,128,256]{3,2,1,0:T(8,128)} %bitcast.48) | data formatting | bytes 33554432 | tf_op jit(solution)/shard_map/reshape | solution.py:110
  224.1 0.0 all-to-all-done
  224.1 12.6 %all-to-all-start.1 = ((f32[64,2,128,256]{3,1,2,0:T(2,128)}), f32[64,2,128,256]{3,1,2,0:T(2,128)}, u32[]{:S(2)}, u32[]{:S(2)}) async-start(f32[64,2,128,256]{3,1,2,0:T(2,128)} %copy.24), calls=%async_computation.1 | async-start | bytes 33554432 | tf_op jit(solution)/shard_map/all_to_all | solution.py:109
  236.7 0.1 subtract_reduce_fusion
  236.8 0.1 sub.48
  236.9 365.2 %all-to-all-done.1 = f32[64,2,128,256]{3,1,2,0:T(2,128)} async-done(((f32[64,2,128,256]{3,1,2,0:T(2,128)}), f32[64,2,128,256]{3,1,2,0:T(2,128)}, u32[]{:S(2)}, u32[]{:S(2)}) %all-to-all-start.1) | async-done | bytes 16777248 | tf_op jit(solution)/shard_map/all_to_all | solution.py:109
  602.2 12.1 %copy.25 = f32[64,2,128,256]{3,1,0,2:T(2,128)} copy(f32[64,2,128,256]{3,1,2,0:T(2,128)} %all-to-all-done.1) | data formatting | bytes 33554432 | tf_op jit(solution)/shard_map/all_to_all | solution.py:109
  614.3 0.0 copy-start.1
  614.3 20.7 %reshape.87 = f32[128,128,256]{2,0,1:T(8,128)} reshape(f32[64,2,128,256]{3,1,0,2:T(2,128)} %copy.25) | data formatting | bytes 33554432 | tf_op jit(solution)/shard_map/reshape | solution.py:124
  635.0 9.4 %fusion.34 = f32[32,128,256]{2,0,1:T(8,128)S(1)} fusion(f32[128,128,256]{2,0,1:T(8,128)} %reshape.87, s32[128]{0:T(128)S(1)} %sub.48), kind=kOutput, calls=%fused_computation.43 | convolution fusion | flops 1610616832 | bytes 20972032 | tf_op jit(solution)/shard_map/bs,sjk->bjk/dot_general | solution.py:123
  644.4 4.4 copy.26
  648.8 0.0 copy-done.1
  (11 shorter events, 0.1 us)
Async XLA Ops:
  6.5 149.4 %copy-start = (bf16[64,128,128]{2,1,0:T(8,128)(2,1)S(1)}, bf16[64,128,128]{2,1,0:T(8,128)(2,1)}, u32[]{:S(2)}) copy-start(bf16[64,128,128]{2,1,0:T(8,128)(2,1)} %param.16) | copy-start | bytes 6291460
  6.5 132.3 %all-gather.3.cloned.1.call-start = ((), (), s32[]{:S(2)}) async-start(), calls=%async_computation.2 | async-start | bytes 7864320 | tf_op jit(solution)/shard_map/all_gather | solution.py:16
  26.3 25.6 %copy-start.3 = (s32[192,1]{0,1:T(1,128)S(1)}, s32[192,1]{0,1:T(1,128)}, u32[]{:S(2)}) copy-start(s32[192,1]{0,1:T(1,128)} %param.12) | copy-start | bytes 2308
  51.2 16.3 %copy-start.4 = (s32[64,1]{0,1:T(1,128)S(1)}, s32[64,1]{0,1:T(1,128)}, u32[]{:S(2)}) copy-start(s32[64,1]{0,1:T(1,128)} %param.18) | copy-start | bytes 772
  51.2 31.3 %copy-start.2 = (s32[65]{0:T(128)S(1)}, s32[65]{0:T(128)}, u32[]{:S(2)}) copy-start(s32[65]{0:T(128)} %param.15) | copy-start | bytes 784
  51.2 33.2 %copy-start.5 = (s32[65]{0:T(128)S(1)}, s32[65]{0:T(128)}, u32[]{:S(2)}) copy-start(s32[65]{0:T(128)} %param.20) | copy-start | bytes 784
  51.2 35.0 %copy-start.6 = (s32[64,1]{0,1:T(1,128)S(1)}, s32[64,1]{0,1:T(1,128)}, u32[]{:S(2)}) copy-start(s32[64,1]{0,1:T(1,128)} %param.17) | copy-start | bytes 772
  69.5 154.6 %all-to-all-start = ((s32[64,1,2]{2,1,0:T(1,128)}), s32[64,1,2]{2,1,0:T(1,128)S(1)}, u32[]{:S(2)}, u32[]{:S(2)}) async-start(s32[64,1,2]{2,1,0:T(1,128)} %bitcast.5), calls=%async_computation | async-start | bytes 65536 | tf_op jit(solution)/shard_map/all_to_all | solution.py:116
  142.3 5.8 collective-permute-start
  224.1 378.1 %all-to-all-start.1 = ((f32[64,2,128,256]{3,1,2,0:T(2,128)}), f32[64,2,128,256]{3,1,2,0:T(2,128)}, u32[]{:S(2)}, u32[]{:S(2)}) async-start(f32[64,2,128,256]{3,1,2,0:T(2,128)} %copy.24), calls=%async_computation.1 | async-start | bytes 33554432 | tf_op jit(solution)/shard_map/all_to_all | solution.py:109
  614.3 34.5 %copy-start.1 = (bf16[64,128,128]{2,1,0:T(8,128)(2,1)S(1)}, bf16[64,128,128]{2,1,0:T(8,128)(2,1)}, u32[]{:S(2)}) copy-start(bf16[64,128,128]{2,1,0:T(8,128)(2,1)} %param.16) | copy-start | bytes 6291460
Sparse Core Ops, SparseCore 0:
  67.0 71.8 all-gather.2
